TPU v7x, 128 devices: a whole 4x4x4 slice. The times are simulated.
128 devices in a mesh: dp: 4 (over y), row: 8 (over z, core), col: 4 (over x).
Axes of the slice: x: 4, y: 4, z: 4, core: 2. Of those that a mesh axis runs over, the one named last changes fastest.
Arguments:
- gradients: bfloat16 [4, 8192, 14336], P('dp', 'row', 'col'), may hold values from -6 to 6
- test_matrix: int32 [14336, 512], P('col'), may hold values from -3 to 3
- old_basis: float32 [8192, 512], P('row'), may hold values from -0.0625 to 0.0625
- first_moment: float32 [512, 14336], P(('dp', 'row'), 'col'), may hold values from -24 to 24
- second_moment: float32 [512, 14336], P(('dp', 'row'), 'col'), may hold values from 1 to 16
Outputs:
- projected: float32 [512, 14336], P(('dp', 'row'), 'col')
- first_moment_new: float32 [512, 14336], P(('dp', 'row'), 'col')
- second_moment_new: float32 [512, 14336], P(('dp', 'row'), 'col')
All inputs are finite; a program needn't handle non-finite values.
Results may differ from a plain program's by a relative error of at most 0.0023.
Values sent between devices are 32-bit elements; how exact they have to be, the bound alone decides.
A program may use at most 128 MiB of HBM per device.

v0:
```python
import jax
import jax.numpy as jnp
from jax import lax
from jax.sharding import PartitionSpec as P

highest = lax.Precision.HIGHEST


def from_partner(value, axis, bit):
    return lax.ppermute(value, axis, [(i, i ^ 1 << bit) for i in range(lax.axis_size(axis))])


def gram_of(row_block):
    return lax.dot_general(
        row_block,
        row_block,
        (((0,), (0,)), ((), ())),
        precision=highest,
        preferred_element_type=jnp.float32,
    )


def basis_from(lower_factor, sketch_part):
    return jax.scipy.linalg.solve_triangular(lower_factor, sketch_part.T, lower=True).T


def local(gradients, test_matrix, old_basis, first_moment, second_moment):
    replica_grad = gradients[0]
    test_values = test_matrix.astype(jnp.bfloat16)
    partial_value = jnp.dot(replica_grad, test_values, preferred_element_type=jnp.float32)
    sketch = lax.psum(partial_value, ("dp", "col"))
    upper_factor = jnp.linalg.cholesky(gram_of(sketch)).T
    for bit_level in range(lax.axis_size("row").bit_length() - 1):
        partner = from_partner(upper_factor, "row", bit_level)
        upper_factor = jnp.linalg.cholesky(gram_of(upper_factor) + gram_of(partner)).T
    new_basis = basis_from(upper_factor.T, sketch)
    basis_low = new_basis.astype(jnp.bfloat16)
    local_correlation = lax.dot_general(
        new_basis,
        old_basis,
        (((0,), (0,)), ((), ())),
        precision=highest,
        preferred_element_type=jnp.float32,
    )
    correlation = lax.psum(local_correlation, "row")
    rank_dev = first_moment.shape[0]
    rank_start = lax.axis_index(("dp", "row")) * rank_dev
    projected = lax.psum_scatter(
        lax.dot_general(
            basis_low, replica_grad, (((0,), (0,)), ((), ())), preferred_element_type=jnp.float32
        ),
        ("dp", "row"),
        scatter_dimension=0,
        tiled=True,
    )
    own_rows = lax.dynamic_slice_in_dim(correlation, rank_start, rank_dev, 0)
    squared = own_rows * own_rows
    turned_first = jnp.dot(
        own_rows,
        lax.all_gather(first_moment, ("dp", "row"), axis=0, tiled=True),
        precision=highest,
        preferred_element_type=jnp.float32,
    )
    turned_second = jnp.dot(
        squared,
        lax.all_gather(second_moment, ("dp", "row"), axis=0, tiled=True),
        precision=highest,
        preferred_element_type=jnp.float32,
    )
    first_new = 0.9 * turned_first + 0.1 * projected
    second_new = 0.95 * turned_second + 0.05 * projected * projected
    return (projected, first_new, second_new)


def solution(mesh):
    in_specs = (
        P("dp", "row", "col"),
        P("col", None),
        P("row", None),
        P(("dp", "row"), "col"),
        P(("dp", "row"), "col"),
    )
    out_specs = (P(("dp", "row"), "col"), P(("dp", "row"), "col"), P(("dp", "row"), "col"))
    return jax.shard_map(local, mesh=mesh, in_specs=in_specs, out_specs=out_specs, check_vma=False)
```

profile of v0, /device:TPU:1, one launch (start us, length us, event | category | flops | bytes accessed | tf_op | source)
XLA Modules:
  0.0 834.7 jit_solution(15446949937610158620)
XLA Ops:
  8.1 10.6 %fusion.2 = f32[1024,512]{1,0:T(8,128)} fusion(bf16[1,1024,3584]{2,1,0:T(8,128)(2,1)} %param.6, s32[3584,512]{1,0:T(8,128)} %param.7), kind=kOutput, calls=%fused_computation.4 | convolution fusion | flops 3759931392 | bytes 16777216 | tf_op jit(solution)/shard_map/dot_general | solution.py:30
  18.9 92.7 %all-reduce.4.cloned.1.call-done = f32[1024,512]{1,0:T(8,128)} async-done(((f32[1024,512]{1,0:T(8,128)}), f32[1024,512]{1,0:T(8,128)}) %all-reduce.4.cloned.1.call-update) | async-done | bytes 2097168 | tf_op jit(solution)/shard_map/psum | solution.py:31
  111.5 5.7 fusion.148
  118.6 1.4 fusion.25
  121.0 11.7 %cholesky.462 = f32[128,128]{1,0:T(8,128)S(1)} custom-call(f32[128,128]{1,0:T(8,128)S(1)} %cholesky.746), custom_call_target="Cholesky" | custom-call | tf_op jit(solution)/shard_map/jit(cholesky)/cholesky | solution.py:32
  132.8 9.8 %custom-call.34 = f32[1,128,128]{1,2,0:T(8,128)S(1)} custom-call(f32[1,128,128]{2,1,0:T(8,128)S(1)} %get-tuple-element.61), custom_call_target="InvertDiagBlocksLowerTriangular" | custom-call | tf_op jit(solution)/shard_map/jit(cholesky)/cholesky | solution.py:32
  145.2 12.1 %cholesky.481 = f32[128,128]{1,0:T(8,128)S(1)} custom-call(f32[128,128]{1,0:T(8,128)S(1)} %cholesky.750), custom_call_target="Cholesky" | custom-call | tf_op jit(solution)/shard_map/jit(cholesky)/cholesky | solution.py:32
  157.4 9.8 %custom-call.35 = f32[1,128,128]{1,2,0:T(8,128)S(1)} custom-call(f32[1,128,128]{2,1,0:T(8,128)S(1)} %get-tuple-element.58), custom_call_target="InvertDiagBlocksLowerTriangular" | custom-call | tf_op jit(solution)/shard_map/jit(cholesky)/cholesky | solution.py:32
  168.8 11.7 %cholesky.502 = f32[128,128]{1,0:T(8,128)S(1)} custom-call(f32[128,128]{1,0:T(8,128)S(1)} %cholesky.755), custom_call_target="Cholesky" | custom-call | tf_op jit(solution)/shard_map/jit(cholesky)/cholesky | solution.py:32
  181.2 9.8 %custom-call.36 = f32[1,128,128]{1,2,0:T(8,128)S(1)} custom-call(f32[1,128,128]{2,1,0:T(8,128)S(1)} %get-tuple-element.55), custom_call_target="InvertDiagBlocksLowerTriangular" | custom-call | tf_op jit(solution)/shard_map/jit(cholesky)/cholesky | solution.py:32
  192.4 11.9 %cholesky.519 = f32[128,128]{1,0:T(8,128)S(1)} custom-call(f32[128,128]{1,0:T(8,128)S(1)} %convolution_subtract_fusion.4), custom_call_target="Cholesky" | custom-call | tf_op jit(solution)/shard_map/jit(cholesky)/cholesky | solution.py:32
  208.3 2.1 collective-permute-start
  210.4 1.9 fusion.27
  212.7 1.9 convolution_add_fusion.2
  215.9 1.4 fusion.24
  218.3 11.7 %cholesky.534 = f32[128,128]{1,0:T(8,128)S(1)} custom-call(f32[128,128]{1,0:T(8,128)S(1)} %cholesky.759), custom_call_target="Cholesky" | custom-call | tf_op jit(solution)/shard_map/jit(cholesky)/cholesky | solution.py:35
  230.2 9.8 %custom-call.37 = f32[1,128,128]{1,2,0:T(8,128)S(1)} custom-call(f32[1,128,128]{2,1,0:T(8,128)S(1)} %get-tuple-element.51), custom_call_target="InvertDiagBlocksLowerTriangular" | custom-call | tf_op jit(solution)/shard_map/jit(cholesky)/cholesky | solution.py:35
  242.5 12.1 %cholesky.553 = f32[128,128]{1,0:T(8,128)S(1)} custom-call(f32[128,128]{1,0:T(8,128)S(1)} %cholesky.763), custom_call_target="Cholesky" | custom-call | tf_op jit(solution)/shard_map/jit(cholesky)/cholesky | solution.py:35
  255.9 9.8 %custom-call.38 = f32[1,128,128]{1,2,0:T(8,128)S(1)} custom-call(f32[1,128,128]{2,1,0:T(8,128)S(1)} %get-tuple-element.48), custom_call_target="InvertDiagBlocksLowerTriangular" | custom-call | tf_op jit(solution)/shard_map/jit(cholesky)/cholesky | solution.py:35
  267.3 11.7 %cholesky.574 = f32[128,128]{1,0:T(8,128)S(1)} custom-call(f32[128,128]{1,0:T(8,128)S(1)} %cholesky.768), custom_call_target="Cholesky" | custom-call | tf_op jit(solution)/shard_map/jit(cholesky)/cholesky | solution.py:35
  279.7 9.8 %custom-call.39 = f32[1,128,128]{1,2,0:T(8,128)S(1)} custom-call(f32[1,128,128]{2,1,0:T(8,128)S(1)} %get-tuple-element.45), custom_call_target="InvertDiagBlocksLowerTriangular" | custom-call | tf_op jit(solution)/shard_map/jit(cholesky)/cholesky | solution.py:35
  289.7 1.4 slice_subtract_fusion.8
  291.1 11.7 %cholesky.591 = f32[128,128]{1,0:T(8,128)S(1)} custom-call(f32[128,128]{1,0:T(8,128)S(1)} %slice_subtract_fusion.8), custom_call_target="Cholesky" | custom-call | tf_op jit(solution)/shard_map/jit(cholesky)/cholesky | solution.py:35
  307.6 1.9 fusion.29
  309.5 21.2 %collective-permute-done.1 = f32[512,512]{0,1:T(8,128)S(1)} collective-permute-done((f32[512,512]{0,1:T(8,128)S(1)}, f32[512,512]{0,1:T(8,128)S(1)}, u32[]{:S(2)}, u32[]{:S(2)}) %collective-permute-start.1) | collective-permute-done | bytes 1048608 | tf_op jit(solution)/shard_map/ppermute | solution.py:10
  330.6 1.9 convolution_add_fusion.1
  333.8 1.4 fusion.23
  336.3 11.7 %cholesky.606 = f32[128,128]{1,0:T(8,128)S(1)} custom-call(f32[128,128]{1,0:T(8,128)S(1)} %cholesky.772), custom_call_target="Cholesky" | custom-call | tf_op jit(solution)/shard_map/jit(cholesky)/cholesky | solution.py:35
  348.2 9.8 %custom-call.40 = f32[1,128,128]{1,2,0:T(8,128)S(1)} custom-call(f32[1,128,128]{2,1,0:T(8,128)S(1)} %get-tuple-element.41), custom_call_target="InvertDiagBlocksLowerTriangular" | custom-call | tf_op jit(solution)/shard_map/jit(cholesky)/cholesky | solution.py:35
  360.5 12.1 %cholesky.625 = f32[128,128]{1,0:T(8,128)S(1)} custom-call(f32[128,128]{1,0:T(8,128)S(1)} %cholesky.776), custom_call_target="Cholesky" | custom-call | tf_op jit(solution)/shard_map/jit(cholesky)/cholesky | solution.py:35
  373.9 9.8 %custom-call.41 = f32[1,128,128]{1,2,0:T(8,128)S(1)} custom-call(f32[1,128,128]{2,1,0:T(8,128)S(1)} %get-tuple-element.38), custom_call_target="InvertDiagBlocksLowerTriangular" | custom-call | tf_op jit(solution)/shard_map/jit(cholesky)/cholesky | solution.py:35
  385.3 11.7 %cholesky.646 = f32[128,128]{1,0:T(8,128)S(1)} custom-call(f32[128,128]{1,0:T(8,128)S(1)} %cholesky.781), custom_call_target="Cholesky" | custom-call | tf_op jit(solution)/shard_map/jit(cholesky)/cholesky | solution.py:35
  397.7 9.8 %custom-call.42 = f32[1,128,128]{1,2,0:T(8,128)S(1)} custom-call(f32[1,128,128]{2,1,0:T(8,128)S(1)} %get-tuple-element.35), custom_call_target="InvertDiagBlocksLowerTriangular" | custom-call | tf_op jit(solution)/shard_map/jit(cholesky)/cholesky | solution.py:35
  407.7 1.4 slice_subtract_fusion.7
  409.1 11.7 %cholesky.663 = f32[128,128]{1,0:T(8,128)S(1)} custom-call(f32[128,128]{1,0:T(8,128)S(1)} %slice_subtract_fusion.7), custom_call_target="Cholesky" | custom-call | tf_op jit(solution)/shard_map/jit(cholesky)/cholesky | solution.py:35
  425.2 2.9 collective-permute-start.2
  428.1 1.9 fusion.31
  430.0 20.5 %collective-permute-done.2 = f32[512,512]{0,1:T(8,128)} collective-permute-done((f32[512,512]{0,1:T(8,128)}, f32[512,512]{0,1:T(8,128)}, u32[]{:S(2)}, u32[]{:S(2)}) %collective-permute-start.2) | collective-permute-done | bytes 1048608 | tf_op jit(solution)/shard_map/ppermute | solution.py:10
  450.5 3.4 convolution_add_fusion
  455.2 1.4 fusion.22
  457.7 11.7 %cholesky.678 = f32[128,128]{1,0:T(8,128)S(1)} custom-call(f32[128,128]{1,0:T(8,128)S(1)} %cholesky.785), custom_call_target="Cholesky" | custom-call | tf_op jit(solution)/shard_map/jit(cholesky)/cholesky | solution.py:35
  469.5 9.8 %custom-call.43 = f32[1,128,128]{1,2,0:T(8,128)S(1)} custom-call(f32[1,128,128]{2,1,0:T(8,128)S(1)} %get-tuple-element.31), custom_call_target="InvertDiagBlocksLowerTriangular" | custom-call | tf_op jit(solution)/shard_map/jit(cholesky)/cholesky | solution.py:35
  481.9 12.1 %cholesky.697 = f32[128,128]{1,0:T(8,128)S(1)} custom-call(f32[128,128]{1,0:T(8,128)S(1)} %cholesky.789), custom_call_target="Cholesky" | custom-call | tf_op jit(solution)/shard_map/jit(cholesky)/cholesky | solution.py:35
  495.3 9.8 %custom-call.44 = f32[1,128,128]{1,2,0:T(8,128)S(1)} custom-call(f32[1,128,128]{2,1,0:T(8,128)S(1)} %get-tuple-element.28), custom_call_target="InvertDiagBlocksLowerTriangular" | custom-call | tf_op jit(solution)/shard_map/jit(cholesky)/cholesky | solution.py:35
  506.7 11.7 %cholesky.718 = f32[128,128]{1,0:T(8,128)S(1)} custom-call(f32[128,128]{1,0:T(8,128)S(1)} %cholesky.794), custom_call_target="Cholesky" | custom-call | tf_op jit(solution)/shard_map/jit(cholesky)/cholesky | solution.py:35
  519.0 9.8 %custom-call.45 = f32[1,128,128]{1,2,0:T(8,128)S(1)} custom-call(f32[1,128,128]{2,1,0:T(8,128)S(1)} %get-tuple-element.25), custom_call_target="InvertDiagBlocksLowerTriangular" | custom-call | tf_op jit(solution)/shard_map/jit(cholesky)/cholesky | solution.py:35
  530.5 11.7 %cholesky.735 = f32[128,128]{1,0:T(8,128)S(1)} custom-call(f32[128,128]{1,0:T(8,128)S(1)} %slice_subtract_fusion.6), custom_call_target="Cholesky" | custom-call | tf_op jit(solution)/shard_map/jit(cholesky)/cholesky | solution.py:35
  546.4 14.0 %while.1 = (s32[]{:T(128)}, f32[512,512]{1,0:T(8,128)}, s32[4,2]{0,1:T(2,128)S(1)}, f32[4,128,128]{2,1,0:T(8,128)}, s32[]{:T(128)}) while((s32[]{:T(128)}, f32[512,512]{1,0:T(8,128)}, s32[4,2]{0,1:T(2,128)S(1)}, f32[4,128,128]{2,1,0:T(8,128)}, s32[]{:T(128)}) %tuple.53), condition=%wide.while_cond, body=%wide.while_body.sunk | while | flops 2 | bytes 132705 | solution.py:24
  547.0 2.9 bitcast_dynamic-update-slice_fusion.2
  550.6 2.9 bitcast_dynamic-update-slice_fusion.2
  554.1 2.9 bitcast_dynamic-update-slice_fusion.2
  557.6 2.8 bitcast_dynamic-update-slice_fusion.2
  560.4 40.1 %custom-call.24 = f32[4,128,128]{1,2,0:T(8,128)S(1)} custom-call(f32[4,128,128]{2,1,0:T(8,128)} %get-tuple-element.11), custom_call_target="InvertDiagBlocksLowerTriangular" | custom-call | tf_op jit(solution)/shard_map/jit(_solve_triangular)/triangular_solve | solution.py:24
  600.6 1.8 fusion.32
  602.4 2.1 convolution_subtract_fusion.1
  605.1 2.7 convolution_subtract_fusion
  608.5 3.8 fusion.13
  613.8 4.5 fusion.16
  619.2 10.3 %fusion = f32[512,3584]{1,0:T(8,128)} fusion(bf16[1,1024,3584]{2,1,0:T(8,128)(2,1)} %param.6, f32[128,1024]{1,0:T(8,128)} %copy-done.7, f32[128,1024]{1,0:T(8,128)} %copy-done.2, f32[128,1024]{1,0:T(8,128)S(1)} %fusion.78, f32[128,1024]{1,0:T(8,128)S(1)} %fusion.32), kind=kOutput, calls=%fused_computation.2 | convolution fusion | flops 3762290688 | bytes 16777216 | tf_op jit(solution)/shard_map/dot_general | solution.py:49
  630.1 55.8 %all-reduce.6.cloned.1.call-done = f32[512,512]{1,0:T(8,128)} async-done(((f32[512,512]{1,0:T(8,128)}), f32[512,512]{1,0:T(8,128)}) %all-reduce.6.cloned.1.call-update) | async-done | bytes 1048592 | tf_op jit(solution)/shard_map/psum | solution.py:45
  685.9 79.3 %reduce-scatter.2.cloned.1.call-done = f32[16,3584]{1,0:T(8,128)} async-done(((f32[512,3584]{1,0:T(8,128)}), f32[16,3584]{1,0:T(8,128)}) %reduce-scatter.2.cloned.1.call-update) | async-done | bytes 229392 | tf_op jit(solution)/shard_map/reduce_scatter | solution.py:48
  765.2 7.4 fusion.4
  772.5 47.0 %all-gather.3.cloned.1.call-done = f32[512,3584]{1,0:T(8,128)} async-done(((f32[16,3584]{1,0:T(8,128)}), f32[512,3584]{1,0:T(8,128)}) %all-gather.3.cloned.1.call-update) | async-done | bytes 7340048 | tf_op jit(solution)/shard_map/all_gather | solution.py:60
  819.5 7.3 fusion.5
  (122 shorter events, 50.6 us)
Async XLA Ops:
  8.0 605.8 %copy-start = (f32[1024,512]{1,0:T(8,128)S(1)}, f32[1024,512]{1,0:T(8,128)}, u32[]{:S(2)}) copy-start(f32[1024,512]{1,0:T(8,128)} %param.8) | copy-start | bytes 6291460
  8.0 103.5 %all-reduce.4.cloned.1.call-start = ((), (), s32[]{:S(2)}) async-start(), calls=%async_computation.1 | async-start | bytes 4194304 | tf_op jit(solution)/shard_map/psum | solution.py:31
  18.6 667.3 %all-reduce.6.cloned.1.call-start = ((), (), s32[]{:S(2)}) async-start(), calls=%async_computation.3 | async-start | bytes 2097152 | tf_op jit(solution)/shard_map/psum | solution.py:45
  120.0 1.0 copy-start.6
  208.3 4.4 collective-permute-start
  217.3 1.0 copy-start.4
  306.2 24.4 %collective-permute-start.1 = (f32[512,512]{0,1:T(8,128)S(1)}, f32[512,512]{0,1:T(8,128)S(1)}, u32[]{:S(2)}, u32[]{:S(2)}) collective-permute-start(f32[512,512]{0,1:T(8,128)S(1)} %fusion.28), channel_id=1, source_target_pairs={{0,8},{4,12},{8,0},{12,4},{16,24},{20,28},{24,16},{28,20},{1,9},{5... | collective-permute-start | bytes 3145736 | tf_op jit(solution)/shard_map/ppermute | solution.py:10
  335.3 1.0 copy-start.5
  425.2 25.3 %collective-permute-start.2 = (f32[512,512]{0,1:T(8,128)}, f32[512,512]{0,1:T(8,128)}, u32[]{:S(2)}, u32[]{:S(2)}) collective-permute-start(f32[512,512]{0,1:T(8,128)} %fusion.30), channel_id=1, source_target_pairs={{0,16},{4,20},{8,24},{12,28},{16,0},{20,4},{24,8},{28,12},{1,17},{... | collective-permute-start | bytes 3145736 | tf_op jit(solution)/shard_map/ppermute | solution.py:10
  456.7 1.0 copy-start.3
  600.5 4.6 copy-start.1
  608.5 4.5 copy-start.2
  613.0 0.8 copy-start.7
  618.4 67.5 %all-gather.5.cloned.1.call-start = ((), (), s32[]{:S(2)}) async-start(), calls=%async_computation.5 | async-start | bytes 7569408 | tf_op jit(solution)/shard_map/all_gather | solution.py:66
  618.9 146.2 %reduce-scatter.2.cloned.1.call-start = ((), (), s32[]{:S(2)}) async-start(), calls=%async_computation.2 | async-start | bytes 7569408 | tf_op jit(solution)/shard_map/reduce_scatter | solution.py:48
  629.6 190.0 %all-gather.3.cloned.1.call-start = ((), (), s32[]{:S(2)}) async-start(), calls=%async_computation.4 | async-start | bytes 7569408 | tf_op jit(solution)/shard_map/all_gather | solution.py:60
  765.2 54.4 %copy-start.8 = (f32[16,3584]{1,0:T(8,128)S(1)}, f32[16,3584]{1,0:T(8,128)}, u32[]{:S(2)}) copy-start(f32[16,3584]{1,0:T(8,128)} %reduce-scatter.2.cloned.1.call-done) | copy-start | bytes 688132
Sparse Core Ops, SparseCore 0:
  18.8 92.7 all-reduce.3
  618.5 67.3 all-reduce.5
Sparse Core Ops, SparseCore 1:
  621.1 53.5 all-gather.4
  678.9 86.3 reduce-scatter.1
  767.3 52.2 all-gather.2
where the time goes:
time: 838 us; the launch traced here: 835 us
  other arithmetic  365 us (44%)
  waiting for transfers between devices  318 us (38%)
  matrix products  93.3 us (11%)
  between operations  26.7 us (3%)
  local copies, waits for them, and re-layouts  24.6 us (3%)
    another operation x45, other arithmetic, local(): jnp.linalg.cholesky(gram_of(upper_factor) + gram_of(partner))  238 us
    psum x1, waiting for transfers between devices, local(): sketch = lax.psum(partial_value, ('dp', 'col'))  92.7 us
    reduce_scatter x1, waiting for transfers between devices, local(): lax.psum_scatter(lax.dot_general(basis_low, replica_grad, (((0,), (0,)),...  79.3 us
    another operation x14, other arithmetic, local(): upper_factor = jnp.linalg.cholesky(gram_of(sketch)).T  78.9 us
    psum x1, waiting for transfers between devices, local(): correlation = lax.psum(local_correlation, 'row')  55.8 us
    all_gather x1, waiting for transfers between devices, local(): lax.all_gather(first_moment, ('dp', 'row'), axis=0, tiled=True)  47 us
    ppermute x3, waiting for transfers between devices, from_partner(): lax.ppermute(value, axis, [(i, i ^ 1 << bit) for i in range(lax.axis_size...  42.1 us
    another operation x3, other arithmetic, basis_from(): jax.scipy.linalg.solve_triangular(lower_factor, sketch_part.T, lower=True)  41.2 us
  transfers between devices with their start and end apart: 8, of which 7 were waited for; matrix products, arithmetic and copies ran while one was open for 3% of the time, Pallas kernels for 0%

commit v1 on v0

--- a/solution.py
+++ b/solution.py
@@ -42,7 +42,7 @@
         precision=highest,
         preferred_element_type=jnp.float32,
     )
-    correlation = lax.psum(local_correlation, "row")
+    correlation = lax.all_gather(local_correlation, "row").sum(axis=0)
     rank_dev = first_moment.shape[0]
     rank_start = lax.axis_index(("dp", "row")) * rank_dev
     projected = lax.psum_scatter(

time: 838 us -> 883 us (1.054)
  waiting for transfers between devices: 318 us -> 361 us
    psum x1 -> x0, waiting for transfers between devices: 55.8 us -> none  [local(): correlation = lax.psum(local_correlation, 'row')]
    all_gather x1, waiting for transfers between devices: 0.01 us -> 48.7 us  [local(): lax.all_gather(second_moment, ('dp', 'row'), axis=0, tiled=True)]
    all_gather x0 -> x1, waiting for transfers between devices: none -> 39.4 us  [local(): correlation = lax.all_gather(local_correlation, 'row').sum(axis=0)]
    reduce_scatter x1, waiting for transfers between devices: 79.3 us -> 89.8 us  [local(): lax.psum_scatter(lax.dot_general(basis_low, replica_grad, (((0,), (0,)),...]
  transfers between devices with their start and end apart: 8 -> 8, of which waited for: 7 -> 8; matrix products, arithmetic and copies ran while one was open for 3% -> 3% of each run, Pallas kernels for 0% -> 0%
where the time goes in v1:
time: 883 us; the launch traced here: 879 us
  other arithmetic  370 us (42%)
  waiting for transfers between devices  361 us (41%)
  matrix products  92.4 us (10%)
  between operations  24.8 us (3%)
  local copies, waits for them, and re-layouts  24.6 us (3%)
    another operation x45, other arithmetic, local(): jnp.linalg.cholesky(gram_of(upper_factor) + gram_of(partner))  238 us
    psum x1, waiting for transfers between devices, local(): sketch = lax.psum(partial_value, ('dp', 'col'))  92.7 us
    reduce_scatter x1, waiting for transfers between devices, local(): lax.psum_scatter(lax.dot_general(basis_low, replica_grad, (((0,), (0,)),...  89.8 us
    another operation x14, other arithmetic, local(): upper_factor = jnp.linalg.cholesky(gram_of(sketch)).T  78.9 us
    all_gather x1, waiting for transfers between devices, local(): lax.all_gather(second_moment, ('dp', 'row'), axis=0, tiled=True)  48.7 us
    all_gather x1, waiting for transfers between devices, local(): lax.all_gather(first_moment, ('dp', 'row'), axis=0, tiled=True)  47 us
    ppermute x3, waiting for transfers between devices, from_partner(): lax.ppermute(value, axis, [(i, i ^ 1 << bit) for i in range(lax.axis_size...  42.1 us
    another operation x3, other arithmetic, basis_from(): jax.scipy.linalg.solve_triangular(lower_factor, sketch_part.T, lower=True)  41.2 us
  transfers between devices with their start and end apart: 8, of which 8 were waited for; matrix products, arithmetic and copies ran while one was open for 3% of the time, Pallas kernels for 0%

profile of v1, /device:TPU:1, one launch (start us, length us, event | category | flops | bytes accessed | tf_op | source)
XLA Modules:
  0.0 879.5 jit_solution(4543384066974148495)
XLA Ops:
  7.2 10.6 %fusion.2 = f32[1024,512]{1,0:T(8,128)} fusion(bf16[1,1024,3584]{2,1,0:T(8,128)(2,1)} %param.6, s32[3584,512]{1,0:T(8,128)} %param.7), kind=kOutput, calls=%fused_computation.4 | convolution fusion | flops 3759931392 | bytes 16777216 | tf_op jit(solution)/shard_map/dot_general | solution.py:30
  18.0 92.7 %all-reduce.3.cloned.1.call-done = f32[1024,512]{1,0:T(8,128)} async-done(((f32[1024,512]{1,0:T(8,128)}), f32[1024,512]{1,0:T(8,128)}) %all-reduce.3.cloned.1.call-update) | async-done | bytes 2097168 | tf_op jit(solution)/shard_map/psum | solution.py:31
  110.7 5.7 fusion.148
  117.7 1.4 fusion.25
  120.2 11.7 %cholesky.462 = f32[128,128]{1,0:T(8,128)S(1)} custom-call(f32[128,128]{1,0:T(8,128)S(1)} %cholesky.746), custom_call_target="Cholesky" | custom-call | tf_op jit(solution)/shard_map/jit(cholesky)/cholesky | solution.py:32
  131.9 9.8 %custom-call.34 = f32[1,128,128]{1,2,0:T(8,128)S(1)} custom-call(f32[1,128,128]{2,1,0:T(8,128)S(1)} %get-tuple-element.61), custom_call_target="InvertDiagBlocksLowerTriangular" | custom-call | tf_op jit(solution)/shard_map/jit(cholesky)/cholesky | solution.py:32
  144.4 12.1 %cholesky.481 = f32[128,128]{1,0:T(8,128)S(1)} custom-call(f32[128,128]{1,0:T(8,128)S(1)} %cholesky.750), custom_call_target="Cholesky" | custom-call | tf_op jit(solution)/shard_map/jit(cholesky)/cholesky | solution.py:32
  156.5 9.8 %custom-call.35 = f32[1,128,128]{1,2,0:T(8,128)S(1)} custom-call(f32[1,128,128]{2,1,0:T(8,128)S(1)} %get-tuple-element.58), custom_call_target="InvertDiagBlocksLowerTriangular" | custom-call | tf_op jit(solution)/shard_map/jit(cholesky)/cholesky | solution.py:32
  167.9 11.7 %cholesky.502 = f32[128,128]{1,0:T(8,128)S(1)} custom-call(f32[128,128]{1,0:T(8,128)S(1)} %cholesky.755), custom_call_target="Cholesky" | custom-call | tf_op jit(solution)/shard_map/jit(cholesky)/cholesky | solution.py:32
  180.3 9.8 %custom-call.36 = f32[1,128,128]{1,2,0:T(8,128)S(1)} custom-call(f32[1,128,128]{2,1,0:T(8,128)S(1)} %get-tuple-element.55), custom_call_target="InvertDiagBlocksLowerTriangular" | custom-call | tf_op jit(solution)/shard_map/jit(cholesky)/cholesky | solution.py:32
  191.6 11.9 %cholesky.519 = f32[128,128]{1,0:T(8,128)S(1)} custom-call(f32[128,128]{1,0:T(8,128)S(1)} %convolution_subtract_fusion.4), custom_call_target="Cholesky" | custom-call | tf_op jit(solution)/shard_map/jit(cholesky)/cholesky | solution.py:32
  207.5 2.1 collective-permute-start
  209.6 1.9 fusion.27
  211.8 1.9 convolution_add_fusion.2
  215.0 1.4 fusion.24
  217.5 11.7 %cholesky.534 = f32[128,128]{1,0:T(8,128)S(1)} custom-call(f32[128,128]{1,0:T(8,128)S(1)} %cholesky.759), custom_call_target="Cholesky" | custom-call | tf_op jit(solution)/shard_map/jit(cholesky)/cholesky | solution.py:35
  229.4 9.8 %custom-call.37 = f32[1,128,128]{1,2,0:T(8,128)S(1)} custom-call(f32[1,128,128]{2,1,0:T(8,128)S(1)} %get-tuple-element.51), custom_call_target="InvertDiagBlocksLowerTriangular" | custom-call | tf_op jit(solution)/shard_map/jit(cholesky)/cholesky | solution.py:35
  241.7 12.1 %cholesky.553 = f32[128,128]{1,0:T(8,128)S(1)} custom-call(f32[128,128]{1,0:T(8,128)S(1)} %cholesky.763), custom_call_target="Cholesky" | custom-call | tf_op jit(solution)/shard_map/jit(cholesky)/cholesky | solution.py:35
  255.1 9.8 %custom-call.38 = f32[1,128,128]{1,2,0:T(8,128)S(1)} custom-call(f32[1,128,128]{2,1,0:T(8,128)S(1)} %get-tuple-element.48), custom_call_target="InvertDiagBlocksLowerTriangular" | custom-call | tf_op jit(solution)/shard_map/jit(cholesky)/cholesky | solution.py:35
  266.5 11.7 %cholesky.574 = f32[128,128]{1,0:T(8,128)S(1)} custom-call(f32[128,128]{1,0:T(8,128)S(1)} %cholesky.768), custom_call_target="Cholesky" | custom-call | tf_op jit(solution)/shard_map/jit(cholesky)/cholesky | solution.py:35
  278.9 9.8 %custom-call.39 = f32[1,128,128]{1,2,0:T(8,128)S(1)} custom-call(f32[1,128,128]{2,1,0:T(8,128)S(1)} %get-tuple-element.45), custom_call_target="InvertDiagBlocksLowerTriangular" | custom-call | tf_op jit(solution)/shard_map/jit(cholesky)/cholesky | solution.py:35
  290.3 11.7 %cholesky.591 = f32[128,128]{1,0:T(8,128)S(1)} custom-call(f32[128,128]{1,0:T(8,128)S(1)} %slice_subtract_fusion.8), custom_call_target="Cholesky" | custom-call | tf_op jit(solution)/shard_map/jit(cholesky)/cholesky | solution.py:35
  306.8 1.9 fusion.29
  308.6 21.2 %collective-permute-done.1 = f32[512,512]{0,1:T(8,128)S(1)} collective-permute-done((f32[512,512]{0,1:T(8,128)S(1)}, f32[512,512]{0,1:T(8,128)S(1)}, u32[]{:S(2)}, u32[]{:S(2)}) %collective-permute-start.1) | collective-permute-done | bytes 1048608 | tf_op jit(solution)/shard_map/ppermute | solution.py:10
  329.8 1.9 convolution_add_fusion.1
  333.0 1.4 fusion.23
  335.5 11.7 %cholesky.606 = f32[128,128]{1,0:T(8,128)S(1)} custom-call(f32[128,128]{1,0:T(8,128)S(1)} %cholesky.772), custom_call_target="Cholesky" | custom-call | tf_op jit(solution)/shard_map/jit(cholesky)/cholesky | solution.py:35
  347.3 9.8 %custom-call.40 = f32[1,128,128]{1,2,0:T(8,128)S(1)} custom-call(f32[1,128,128]{2,1,0:T(8,128)S(1)} %get-tuple-element.41), custom_call_target="InvertDiagBlocksLowerTriangular" | custom-call | tf_op jit(solution)/shard_map/jit(cholesky)/cholesky | solution.py:35
  359.7 12.1 %cholesky.625 = f32[128,128]{1,0:T(8,128)S(1)} custom-call(f32[128,128]{1,0:T(8,128)S(1)} %cholesky.776), custom_call_target="Cholesky" | custom-call | tf_op jit(solution)/shard_map/jit(cholesky)/cholesky | solution.py:35
  373.1 9.8 %custom-call.41 = f32[1,128,128]{1,2,0:T(8,128)S(1)} custom-call(f32[1,128,128]{2,1,0:T(8,128)S(1)} %get-tuple-element.38), custom_call_target="InvertDiagBlocksLowerTriangular" | custom-call | tf_op jit(solution)/shard_map/jit(cholesky)/cholesky | solution.py:35
  384.5 11.7 %cholesky.646 = f32[128,128]{1,0:T(8,128)S(1)} custom-call(f32[128,128]{1,0:T(8,128)S(1)} %cholesky.781), custom_call_target="Cholesky" | custom-call | tf_op jit(solution)/shard_map/jit(cholesky)/cholesky | solution.py:35
  396.9 9.8 %custom-call.42 = f32[1,128,128]{1,2,0:T(8,128)S(1)} custom-call(f32[1,128,128]{2,1,0:T(8,128)S(1)} %get-tuple-element.35), custom_call_target="InvertDiagBlocksLowerTriangular" | custom-call | tf_op jit(solution)/shard_map/jit(cholesky)/cholesky | solution.py:35
  408.3 11.7 %cholesky.663 = f32[128,128]{1,0:T(8,128)S(1)} custom-call(f32[128,128]{1,0:T(8,128)S(1)} %slice_subtract_fusion.7), custom_call_target="Cholesky" | custom-call | tf_op jit(solution)/shard_map/jit(cholesky)/cholesky | solution.py:35
  424.4 2.9 collective-permute-start.2
  427.3 1.9 fusion.31
  429.1 20.5 %collective-permute-done.2 = f32[512,512]{0,1:T(8,128)} collective-permute-done((f32[512,512]{0,1:T(8,128)}, f32[512,512]{0,1:T(8,128)}, u32[]{:S(2)}, u32[]{:S(2)}) %collective-permute-start.2) | collective-permute-done | bytes 1048608 | tf_op jit(solution)/shard_map/ppermute | solution.py:10
  449.7 3.4 convolution_add_fusion
  454.4 1.4 fusion.22
  456.8 11.7 %cholesky.678 = f32[128,128]{1,0:T(8,128)S(1)} custom-call(f32[128,128]{1,0:T(8,128)S(1)} %cholesky.785), custom_call_target="Cholesky" | custom-call | tf_op jit(solution)/shard_map/jit(cholesky)/cholesky | solution.py:35
  468.7 9.8 %custom-call.43 = f32[1,128,128]{1,2,0:T(8,128)S(1)} custom-call(f32[1,128,128]{2,1,0:T(8,128)S(1)} %get-tuple-element.31), custom_call_target="InvertDiagBlocksLowerTriangular" | custom-call | tf_op jit(solution)/shard_map/jit(cholesky)/cholesky | solution.py:35
  481.0 12.1 %cholesky.697 = f32[128,128]{1,0:T(8,128)S(1)} custom-call(f32[128,128]{1,0:T(8,128)S(1)} %cholesky.789), custom_call_target="Cholesky" | custom-call | tf_op jit(solution)/shard_map/jit(cholesky)/cholesky | solution.py:35
  494.5 9.8 %custom-call.44 = f32[1,128,128]{1,2,0:T(8,128)S(1)} custom-call(f32[1,128,128]{2,1,0:T(8,128)S(1)} %get-tuple-element.28), custom_call_target="InvertDiagBlocksLowerTriangular" | custom-call | tf_op jit(solution)/shard_map/jit(cholesky)/cholesky | solution.py:35
  505.8 11.7 %cholesky.718 = f32[128,128]{1,0:T(8,128)S(1)} custom-call(f32[128,128]{1,0:T(8,128)S(1)} %cholesky.794), custom_call_target="Cholesky" | custom-call | tf_op jit(solution)/shard_map/jit(cholesky)/cholesky | solution.py:35
  518.2 9.8 %custom-call.45 = f32[1,128,128]{1,2,0:T(8,128)S(1)} custom-call(f32[1,128,128]{2,1,0:T(8,128)S(1)} %get-tuple-element.25), custom_call_target="InvertDiagBlocksLowerTriangular" | custom-call | tf_op jit(solution)/shard_map/jit(cholesky)/cholesky | solution.py:35
  529.6 11.7 %cholesky.735 = f32[128,128]{1,0:T(8,128)S(1)} custom-call(f32[128,128]{1,0:T(8,128)S(1)} %slice_subtract_fusion.6), custom_call_target="Cholesky" | custom-call | tf_op jit(solution)/shard_map/jit(cholesky)/cholesky | solution.py:35
  545.6 14.0 %while.1 = (s32[]{:T(128)}, f32[512,512]{1,0:T(8,128)}, s32[4,2]{0,1:T(2,128)S(1)}, f32[4,128,128]{2,1,0:T(8,128)}, s32[]{:T(128)}) while((s32[]{:T(128)}, f32[512,512]{1,0:T(8,128)}, s32[4,2]{0,1:T(2,128)S(1)}, f32[4,128,128]{2,1,0:T(8,128)}, s32[]{:T(128)}) %tuple.53), condition=%wide.while_cond, body=%wide.while_body.sunk | while | flops 2 | bytes 132705 | solution.py:24
  546.2 2.9 bitcast_dynamic-update-slice_fusion.2
  549.7 2.9 bitcast_dynamic-update-slice_fusion.2
  553.2 2.9 bitcast_dynamic-update-slice_fusion.2
  556.7 2.8 bitcast_dynamic-update-slice_fusion.2
  559.6 40.1 %custom-call.24 = f32[4,128,128]{1,2,0:T(8,128)S(1)} custom-call(f32[4,128,128]{2,1,0:T(8,128)} %get-tuple-element.11), custom_call_target="InvertDiagBlocksLowerTriangular" | custom-call | tf_op jit(solution)/shard_map/jit(_solve_triangular)/triangular_solve | solution.py:24
  599.7 1.8 fusion.32
  601.6 2.1 convolution_subtract_fusion.1
  604.3 2.7 convolution_subtract_fusion
  607.7 3.8 fusion.13
  613.0 4.5 fusion.16
  618.5 10.5 %fusion = f32[512,3584]{1,0:T(8,128)} fusion(bf16[1,1024,3584]{2,1,0:T(8,128)(2,1)} %param.6, f32[128,1024]{1,0:T(8,128)} %copy-done.7, f32[128,1024]{1,0:T(8,128)} %copy-done.2, f32[128,1024]{1,0:T(8,128)S(1)} %fusion.78, f32[128,1024]{1,0:T(8,128)S(1)} %fusion.32), kind=kOutput, calls=%fused_computation.2 | convolution fusion | flops 3762290688 | bytes 16777216 | tf_op jit(solution)/shard_map/dot_general | solution.py:49
  629.6 39.4 %all-gather.9.cloned.1.call-done = f32[4096,512]{1,0:T(8,128)} async-done(((f32[512,512]{1,0:T(8,128)}), f32[4096,512]{1,0:T(8,128)}) %all-gather.9.cloned.1.call-update) | async-done | bytes 8388624 | tf_op jit(solution)/shard_map/all_gather | solution.py:45
  668.9 4.5 reduce_sum.9
  673.4 48.7 %all-gather.7.cloned.1.call-done = f32[512,3584]{1,0:T(8,128)} async-done(((f32[16,3584]{1,0:T(8,128)}), f32[512,3584]{1,0:T(8,128)}) %all-gather.7.cloned.1.call-update) | async-done | bytes 7340048 | tf_op jit(solution)/shard_map/all_gather | solution.py:66
  722.2 89.8 %reduce-scatter.2.cloned.1.call-done = f32[16,3584]{1,0:T(8,128)} async-done(((f32[512,3584]{1,0:T(8,128)}), f32[16,3584]{1,0:T(8,128)}) %reduce-scatter.2.cloned.1.call-update) | async-done | bytes 229392 | tf_op jit(solution)/shard_map/reduce_scatter | solution.py:48
  812.0 7.4 fusion.4
  819.4 47.0 %all-gather.5.cloned.1.call-done = f32[512,3584]{1,0:T(8,128)} async-done(((f32[16,3584]{1,0:T(8,128)}), f32[512,3584]{1,0:T(8,128)}) %all-gather.5.cloned.1.call-update) | async-done | bytes 7340048 | tf_op jit(solution)/shard_map/all_gather | solution.py:60
  866.3 6.4 fusion.5
  (123 shorter events, 53.5 us)
Async XLA Ops:
  7.2 605.8 %copy-start = (f32[1024,512]{1,0:T(8,128)S(1)}, f32[1024,512]{1,0:T(8,128)}, u32[]{:S(2)}) copy-start(f32[1024,512]{1,0:T(8,128)} %param.8) | copy-start | bytes 6291460
  7.2 103.5 %all-reduce.3.cloned.1.call-start = ((), (), s32[]{:S(2)}) async-start(), calls=%async_computation.1 | async-start | bytes 4194304 | tf_op jit(solution)/shard_map/psum | solution.py:31
  17.8 651.1 %all-gather.9.cloned.1.call-start = ((), (), s32[]{:S(2)}) async-start(), calls=%async_computation.5 | async-start | bytes 9437184 | tf_op jit(solution)/shard_map/all_gather | solution.py:45
  119.2 1.0 copy-start.6
  207.5 4.4 collective-permute-start
  216.5 1.0 copy-start.3
  305.4 24.4 %collective-permute-start.1 = (f32[512,512]{0,1:T(8,128)S(1)}, f32[512,512]{0,1:T(8,128)S(1)}, u32[]{:S(2)}, u32[]{:S(2)}) collective-permute-start(f32[512,512]{0,1:T(8,128)S(1)} %fusion.28), channel_id=1, source_target_pairs={{0,8},{4,12},{8,0},{12,4},{16,24},{20,28},{24,16},{28,20},{1,9},{5... | collective-permute-start | bytes 3145736 | tf_op jit(solution)/shard_map/ppermute | solution.py:10
  334.5 1.0 copy-start.4
  424.4 25.3 %collective-permute-start.2 = (f32[512,512]{0,1:T(8,128)}, f32[512,512]{0,1:T(8,128)}, u32[]{:S(2)}, u32[]{:S(2)}) collective-permute-start(f32[512,512]{0,1:T(8,128)} %fusion.30), channel_id=1, source_target_pairs={{0,16},{4,20},{8,24},{12,28},{16,0},{20,4},{24,8},{28,12},{1,17},{... | collective-permute-start | bytes 3145736 | tf_op jit(solution)/shard_map/ppermute | solution.py:10
  455.8 1.0 copy-start.5
  599.7 4.6 copy-start.1
  607.7 4.5 copy-start.2
  612.2 0.8 copy-start.7
  617.5 104.7 %all-gather.7.cloned.1.call-start = ((), (), s32[]{:S(2)}) async-start(), calls=%async_computation.4 | async-start | bytes 7569408 | tf_op jit(solution)/shard_map/all_gather | solution.py:66
  618.2 193.7 %reduce-scatter.2.cloned.1.call-start = ((), (), s32[]{:S(2)}) async-start(), calls=%async_computation.2 | async-start | bytes 7569408 | tf_op jit(solution)/shard_map/reduce_scatter | solution.py:48
  629.0 237.3 %all-gather.5.cloned.1.call-start = ((), (), s32[]{:S(2)}) async-start(), calls=%async_computation.3 | async-start | bytes 7569408 | tf_op jit(solution)/shard_map/all_gather | solution.py:60
  812.0 54.3 %copy-start.8 = (f32[16,3584]{1,0:T(8,128)S(1)}, f32[16,3584]{1,0:T(8,128)}, u32[]{:S(2)}) copy-start(f32[16,3584]{1,0:T(8,128)} %reduce-scatter.2.cloned.1.call-done) | copy-start | bytes 688132
Sparse Core Ops, SparseCore 0:
  17.9 92.7 all-reduce.2
  617.6 51.2 all-gather.8
  671.2 50.9 all-gather.6
  726.4 85.5 reduce-scatter.1
  814.1 52.1 all-gather.4
